TPU v7x, 128 devices: a whole 4x4x4 slice. The times are simulated.
128 devices in a mesh: req: 32 (over x, y, core), mlp: 4 (over z).
Axes of the slice: x: 4, y: 4, z: 4, core: 2. Of those that a mesh axis runs over, the one named last changes fastest.
Arguments:
- tokens: bfloat16 [1024, 2048], P('req'), may hold values from -6 to 6
- prefix_len: int32 [32], replicated, may hold values from 1 to 4096, 65536 in all
- tail_len: int32 [32, 16], replicated, may hold values from 1 to 64, 512 in all within a row
- tail_src: int32 [512], replicated, may hold values from 0 to 31, as said below
- prefix_kv: bfloat16 [32, 2, 4096, 2048], P('req', None, None, 'mlp'), may hold values from -256 to 256, as said below
- tail_kv: bfloat16 [512, 2, 64, 2048], P('req', None, None, 'mlp'), may hold values from -256 to 256, as said below
- w_qkv: bfloat16 [2048, 3, 2048], P(None, None, 'mlp'), may hold values from -0.125 to 0.125
- w_out: bfloat16 [2048, 2048], P('mlp'), may hold values from -0.125 to 0.125
- w_gate: bfloat16 [8192, 2048], P(('req', 'mlp')), may hold values from -0.125 to 0.125
- w_up: bfloat16 [8192, 2048], P(('req', 'mlp')), may hold values from -0.125 to 0.125
- w_down: bfloat16 [8192, 2048], P(('req', 'mlp')), may hold values from -0.0625 to 0.0625
- w_score: float32 [2048], replicated, may hold values from -0.125 to 0.125
Outputs:
- layer_out: bfloat16 [1024, 2048], P(('req', 'mlp'))
- score: float32 [1024], P(('req', 'mlp'))
Inputs may be any that keep to these rules, and one draw needn't show every extreme that they name: tail_src[c] is the req index whose shard of tail_kv holds the tail of continuation c; each device holds 16 tails, in increasing order of continuation. The 16 continuations of a prompt come in groups of 1 from 16 different devices, so from one device to the device of one prompt goes exactly one tail or none. `prefix_kv`: keys are already rotated. `tail_kv`: keys are already rotated.
All inputs are finite; a program needn't handle non-finite values.
Results may differ from a plain program's by a relative error of at most 0.027.
Values may be sent and summed in bfloat16 or wider, within the bound.
A program may use at most 128 MiB of HBM per device.

v0:
```python
from functools import reduce

import jax
import jax.numpy as jnp
from jax import lax
from jax.sharding import PartitionSpec as P

HEAD_DIM = 128
CONT = 16
NEW = 2


def layer_norm(values):
    centre = values - jnp.mean(values, axis=-1, keepdims=True)
    spread = jnp.mean(centre * centre, axis=-1, keepdims=True)
    return centre * lax.rsqrt(spread + 1e-05)


def rotate(vectors, positions):
    half_dim = vectors.shape[-1] // 2
    exponent = jnp.arange(half_dim, dtype=jnp.float32) * (2.0 / vectors.shape[-1])
    frequency = jnp.power(10000.0, -exponent)
    phase_radians = positions.astype(jnp.float32)[:, None] * frequency[None, :]
    cosine = jnp.cos(phase_radians)[:, None, :]
    sine_part = jnp.sin(phase_radians)[:, None, :]
    leading = vectors[..., :half_dim]
    trailing = vectors[..., half_dim:]
    return jnp.concatenate(
        [leading * cosine - trailing * sine_part, trailing * cosine + leading * sine_part], axis=-1
    )


def attend(queries, key_rows, values, key_mask):
    scaling = queries.shape[-1] ** (-0.5)
    scores = (
        jnp.einsum("cjhe,ckhe->cjhk", queries, key_rows, preferred_element_type=jnp.float32)
        * scaling
    )
    scores = jnp.where(key_mask, scores, -1e30)
    row_max = jnp.max(scores, axis=-1)
    weights = jnp.where(key_mask, jnp.exp(scores - row_max[..., None]), 0.0)
    row_sum = jnp.sum(weights, axis=-1)
    output = jnp.einsum(
        "cjhk,ckhe->cjhe", weights.astype(jnp.bfloat16), values, preferred_element_type=jnp.float32
    )
    return (row_max, row_sum, output)


def tail_attend(queries, cache_rows, lengths):
    local_heads = queries.shape[2]
    shaped = (cache_rows.shape[0], cache_rows.shape[2], local_heads, HEAD_DIM)
    key_rows = cache_rows[:, 0].reshape(shaped)
    value_rows = cache_rows[:, 1].reshape(shaped)
    tail_mask = (jnp.arange(cache_rows.shape[2], dtype=jnp.int32)[None, :] < lengths[:, None])[
        :, None, None, :
    ]
    return attend(queries, key_rows, value_rows, tail_mask)


def combine(pieces):
    overall = reduce(jnp.maximum, [piece[0] for piece in pieces])
    numerator = jnp.zeros_like(pieces[0][2])
    denominator = jnp.zeros_like(pieces[0][1])
    for piece in pieces:
        scale_factor = jnp.exp(piece[0] - overall)
        numerator = numerator + scale_factor[..., None] * piece[2]
        denominator = denominator + scale_factor * piece[1]
    return numerator / denominator[..., None]


def swiglu(normed, gate_rows, up_rows, down_rows):
    contract = (((1,), (1,)), ((), ()))
    gate_out = lax.dot_general(normed, gate_rows, contract, preferred_element_type=jnp.float32)
    up_out = lax.dot_general(normed, up_rows, contract, preferred_element_type=jnp.float32)
    hidden = (jax.nn.silu(gate_out) * up_out).astype(jnp.bfloat16)
    return jnp.dot(hidden, down_rows, preferred_element_type=jnp.float32)


def on_device(
    tokens,
    prefix_len,
    tail_len,
    tail_src,
    prefix_kv,
    tail_kv,
    w_qkv,
    w_out,
    w_gate,
    w_up,
    w_down,
    w_score,
):
    req_index = lax.axis_index("req")
    req_count = lax.axis_size("req")
    cap_rows = max(1, CONT // req_count)
    tok_count = tokens.shape[0]
    head_width = w_qkv.shape[2]
    local_heads = head_width // HEAD_DIM
    prefix_size = prefix_kv.shape[2]
    grouped = (CONT, NEW, local_heads, HEAD_DIM)
    normed = layer_norm(tokens.astype(jnp.float32)).astype(jnp.bfloat16)
    projected = jnp.einsum("td,dcf->tcf", normed, w_qkv, preferred_element_type=jnp.float32)
    own_prefix = lax.dynamic_index_in_dim(prefix_len, req_index, 0, keepdims=False)
    own_tails = lax.dynamic_index_in_dim(tail_len, req_index, 0, keepdims=False)
    offsets = jnp.arange(NEW, dtype=jnp.int32)
    positions = (own_prefix + own_tails[:, None] + offsets[None, :]).reshape(-1)
    queries = rotate(projected[:, 0].reshape(tok_count, local_heads, HEAD_DIM), positions).astype(
        jnp.bfloat16
    )
    new_keys = rotate(projected[:, 1].reshape(tok_count, local_heads, HEAD_DIM), positions).astype(
        jnp.bfloat16
    )
    new_values = projected[:, 2].astype(jnp.bfloat16)
    prefix_keys = prefix_kv[0, 0].reshape(1, prefix_size, local_heads, HEAD_DIM)
    prefix_values = prefix_kv[0, 1].reshape(1, prefix_size, local_heads, HEAD_DIM)
    prefix_mask = (jnp.arange(prefix_size, dtype=jnp.int32) < own_prefix)[None, None, None, :]
    prefix_part = attend(
        queries.reshape(1, tok_count, local_heads, HEAD_DIM),
        prefix_keys,
        prefix_values,
        prefix_mask,
    )
    prefix_part = tuple((member.reshape((CONT, NEW) + member.shape[2:]) for member in prefix_part))
    conts_all = tail_src.shape[0]
    indices = jnp.arange(conts_all, dtype=jnp.int32)
    owners = indices // CONT
    paired = (
        (tail_src[None, :] == tail_src[:, None])
        & (owners[None, :] == owners[:, None])
        & (indices[None, :] < indices[:, None])
    )
    pair_rank = jnp.sum(paired.astype(jnp.int32), axis=1)
    held_ids = jnp.nonzero(tail_src == req_index, size=CONT)[0].astype(jnp.int32)
    send_slots = owners[held_ids] * cap_rows + pair_rank[held_ids]
    own_ids = req_index * CONT + jnp.arange(CONT, dtype=jnp.int32)
    recv_slots = tail_src[own_ids] * cap_rows + pair_rank[own_ids]
    slots_total = req_count * cap_rows
    outgoing = (
        jnp.zeros((slots_total,) + tail_kv.shape[1:], jnp.bfloat16).at[send_slots].set(tail_kv)
    )
    incoming = lax.all_to_all(outgoing, "req", split_axis=0, concat_axis=0, tiled=True)
    fetched = incoming[recv_slots]
    tail_part = tail_attend(queries.reshape(grouped), fetched, own_tails)
    new_mask = (offsets[:, None] >= offsets[None, :])[None, :, None, :]
    new_part = attend(
        queries.reshape(grouped), new_keys.reshape(grouped), new_values.reshape(grouped), new_mask
    )
    attn_mix = (
        combine([prefix_part, tail_part, new_part])
        .reshape(tok_count, head_width)
        .astype(jnp.bfloat16)
    )
    partial_value = jnp.dot(attn_mix, w_out, preferred_element_type=jnp.float32)
    summed = lax.psum(partial_value, "mlp")
    residual = (tokens.astype(jnp.float32) + summed).astype(jnp.bfloat16)
    normed_mid = layer_norm(residual.astype(jnp.float32)).astype(jnp.bfloat16)
    row_share = tok_count // lax.axis_size("mlp")
    mlp_index = lax.axis_index("mlp")
    collected_entries = lax.all_gather(normed_mid, "req", axis=0, tiled=True)
    mlp_sum = lax.psum_scatter(
        swiglu(collected_entries, w_gate, w_up, w_down),
        ("req", "mlp"),
        scatter_dimension=0,
        tiled=True,
    )
    own_rows = lax.dynamic_slice_in_dim(residual, mlp_index * row_share, row_share, 0)
    layer_f32 = own_rows.astype(jnp.float32) + mlp_sum
    layer_out = layer_f32.astype(jnp.bfloat16)
    score = jnp.sum(layer_norm(layer_f32) * w_score[None, :], axis=-1)
    return (layer_out, score)


def solution(mesh):
    in_specs = (
        P("req", None),
        P(),
        P(),
        P(),
        P("req", None, None, "mlp"),
        P("req", None, None, "mlp"),
        P(None, None, "mlp"),
        P("mlp", None),
        P(("req", "mlp"), None),
        P(("req", "mlp"), None),
        P(("req", "mlp"), None),
        P(),
    )
    out_specs = (P(("req", "mlp"), None), P(("req", "mlp")))
    return jax.shard_map(
        on_device, mesh=mesh, in_specs=in_specs, out_specs=out_specs, check_vma=False
    )
```

profile of v0, /device:TPU:0, one launch (start us, length us, event | category | flops | bytes accessed | tf_op | source)
XLA Modules:
  0.0 868.9 jit_solution(6250330086719967981)
XLA Ops:
  7.2 1.5 convert_reduce_fusion.3
  8.7 1.1 convert_reduce_fusion
  9.7 0.3 reduce-window.12
  10.2 0.1 slice_reduce_fusion
  10.4 4.1 scatter_custom_fusion
  14.6 0.8 fusion.58
  15.3 0.7 gather_fusion
  16.0 0.7 gather_fusion.1
  16.8 0.1 fusion.59
  16.9 2.4 broadcast_in_dim.121
  19.3 5.9 scatter_fusion
  25.3 7.7 all-to-all-start
  33.1 0.1 fusion.60
  33.2 0.7 gather_fusion.3
  33.8 0.7 gather_fusion.2
  34.5 0.6 dynamic_slice.11
  35.1 0.2 dynamic-slice_reduce_fusion
  35.3 0.1 convert_reduce_fusion.1
  35.4 0.2 fusion.23
  35.7 0.7 broadcast_add_fusion.1
  36.5 4.0 fusion.34
  40.6 0.1 multiply_cosine_fusion
  40.7 0.1 fusion.81
  41.0 0.1 pad_maximum_fusion
  41.2 0.3 fusion.50
  41.4 0.1 copy.193
  41.7 0.7 fusion.67
  42.4 0.1 copy.206
  42.5 5.7 fusion.78
  48.2 6.4 copy.222
  54.6 0.7 iota_compare_fusion.1
  55.3 4.4 fusion.84
  59.7 0.1 copy.176
  59.8 2.1 fusion.3
  62.0 0.1 copy.209
  62.2 6.4 copy.225
  68.6 0.1 fusion.61
  68.8 0.2 fusion.52
  69.0 4.4 fusion.10
  73.4 12.4 %all-to-all-done = bf16[32,2,64,512]{3,2,1,0:T(8,128)(2,1)} async-done(((bf16[32,2,64,512]{3,2,1,0:T(8,128)(2,1)}), bf16[32,2,64,512]{3,2,1,0:T(8,128)(2,1)}, u32[]{:S(2)}, u32[]{:S(2)}) %all-to-all-start) | async-done | bytes 4194336 | tf_op jit(solution)/shard_map/all_to_all | solution.py:141
  85.8 4.2 gather_fusion.4
  90.0 2.7 fusion.79
  92.7 2.2 reshape_squeeze.15
  94.9 2.0 fusion.83
  96.8 0.1 copy.188
  96.9 0.9 fusion.66
  97.9 0.7 copy.210
  98.6 1.1 reshape_squeeze.17
  99.7 1.7 fusion.12
  101.4 0.7 multiply_add_fusion
  102.1 0.1 fusion.41
  102.3 1.2 fusion.43
  103.6 43.6 %all-reduce.2.cloned.1.call-done = f32[32,2048]{1,0:T(8,128)} async-done(((f32[32,2048]{1,0:T(8,128)}), f32[32,2048]{1,0:T(8,128)}) %all-reduce.2.cloned.1.call-update) | async-done | bytes 262160 | tf_op jit(solution)/shard_map/psum | solution.py:154
  147.1 1.1 convert_reduce_fusion.2
  148.2 0.2 fusion.25
  148.5 0.7 fusion.26
  149.2 0.2 reduce-scatter.2.cloned.1.call-start
  149.5 46.5 %all-gather.2.cloned.1.call-done = bf16[1024,2048]{1,0:T(8,128)(2,1)} async-done(((bf16[32,2048]{1,0:T(8,128)(2,1)}), bf16[1024,2048]{1,0:T(8,128)(2,1)}) %all-gather.2.cloned.1.call-update) | async-done | bytes 4194320 | tf_op jit(solution)/shard_map/all_gather | solution.py:159
  195.9 3.6 fusion.85
  199.5 8.0 fusion.6
  207.5 650.7 %reduce-scatter.2.cloned.1.call-done = f32[8,2048]{1,0:T(8,128)} async-done(((f32[1024,2048]{1,0:T(8,128)}), f32[8,2048]{1,0:T(8,128)}) %reduce-scatter.2.cloned.1.call-update) | async-done | bytes 65552 | tf_op jit(solution)/shard_map/reduce_scatter | solution.py:160
  858.2 1.0 fusion.75
  859.2 1.0 multiply_reduce_fusion.1
  860.2 2.1 multiply_reduce_fusion
  (62 shorter events, 1.4 us)
Async XLA Ops:
  7.2 95.1 %copy-start = (bf16[512,2048]{1,0:T(8,128)(2,1)S(1)}, bf16[512,2048]{1,0:T(8,128)(2,1)}, u32[]{:S(2)}) copy-start(bf16[512,2048]{1,0:T(8,128)(2,1)} %param.19) | copy-start | bytes 6291460
  25.3 8.6 copy-start.1
  25.3 9.2 %copy-start.9 = (s32[32]{0:T(128)S(1)}, s32[32]{0:T(128)}, u32[]{:S(2)}) copy-start(s32[32]{0:T(128)} %param.13) | copy-start | bytes 388
  25.3 9.8 %copy-start.8 = (s32[32,16]{0,1:T(8,128)S(1)}, s32[32,16]{0,1:T(8,128)}, u32[]{:S(2)}) copy-start(s32[32,16]{0,1:T(8,128)} %param.14) | copy-start | bytes 6148
  25.3 10.0 %copy-start.2 = (bf16[32,2048]{1,0:T(8,128)(2,1)S(1)}, bf16[32,2048]{1,0:T(8,128)(2,1)}, u32[]{:S(2)}) copy-start(bf16[32,2048]{1,0:T(8,128)(2,1)} %param.12) | copy-start | bytes 393220
  25.3 60.5 %all-to-all-start = ((bf16[32,2,64,512]{3,2,1,0:T(8,128)(2,1)}), bf16[32,2,64,512]{3,2,1,0:T(8,128)(2,1)}, u32[]{:S(2)}, u32[]{:S(2)}) async-start(bf16[32,2,64,512]{3,2,1,0:T(8,128)(2,1)} %scatter_fusion), calls=%async_computation | async-start | bytes 8388608 | tf_op jit(solution)/shard_map/all_to_all | solution.py:141
  33.0 114.2 %all-reduce.2.cloned.1.call-start = ((), (), s32[]{:S(2)}) async-start(), calls=%async_computation.2 | async-start | bytes 524288 | tf_op jit(solution)/shard_map/psum | solution.py:154
  68.8 26.1 %copy-start.6 = (pred[16,64]{1,0:T(8,128)(4,1)}, pred[16,64]{1,0:T(8,128)(4,1)S(1)}, u32[]{:S(2)}) copy-start(pred[16,64]{1,0:T(8,128)(4,1)S(1)} %iota_compare_fusion.3) | copy-start | bytes 3076
  99.7 96.2 %copy-start.3 = (bf16[64,2048]{1,0:T(8,128)(2,1)S(1)}, bf16[64,2048]{1,0:T(8,128)(2,1)}, u32[]{:S(2)}) copy-start(bf16[64,2048]{1,0:T(8,128)(2,1)} %param.20) | copy-start | bytes 786436
  102.3 97.2 %copy-start.4 = (bf16[64,2048]{1,0:T(8,128)(2,1)S(1)}, bf16[64,2048]{1,0:T(8,128)(2,1)}, u32[]{:S(2)}) copy-start(bf16[64,2048]{1,0:T(8,128)(2,1)} %param.22) | copy-start | bytes 786436
  102.3 97.2 %copy-start.5 = (bf16[64,2048]{1,0:T(8,128)(2,1)S(1)}, bf16[64,2048]{1,0:T(8,128)(2,1)}, u32[]{:S(2)}) copy-start(bf16[64,2048]{1,0:T(8,128)(2,1)} %param.21) | copy-start | bytes 786436
  103.5 92.4 %all-gather.2.cloned.1.call-start = ((), (), s32[]{:S(2)}) async-start(), calls=%async_computation.3 | async-start | bytes 4325376 | tf_op jit(solution)/shard_map/all_gather | solution.py:159
  149.2 709.0 %reduce-scatter.2.cloned.1.call-start = ((), (), s32[]{:S(2)}) async-start(), calls=%async_computation.4 | async-start | bytes 8454144 | tf_op jit(solution)/shard_map/reduce_scatter | solution.py:160
  207.5 652.7 %copy-start.7 = (f32[2048]{0:T(1024)S(1)}, f32[2048]{0:T(1024)}, u32[]{:S(2)}) copy-start(f32[2048]{0:T(1024)} %param.23) | copy-start | bytes 24580
Sparse Core Ops, SparseCore 0:
  103.6 43.4 all-reduce.1
  149.7 46.2 all-gather.1
  207.6 650.5 reduce-scatter.1
where the time goes:
time: 870 us; the launch traced here: 869 us
  waiting for transfers between devices  753 us (87%)
  local copies, waits for them, and re-layouts  42.8 us (5%)
  matrix products  29.6 us (3%)
  other arithmetic  21.2 us (2%)
  between operations  14 us (2%)
    reduce_scatter x1, waiting for transfers between devices, on_device(): lax.psum_scatter(swiglu(collected_entries, w_gate, w_up, w_down), ('req',...  651 us
    all_gather x1, waiting for transfers between devices, on_device(): collected_entries = lax.all_gather(normed_mid, 'req', axis=0, tiled=True)  46.5 us
    psum x1, waiting for transfers between devices, on_device(): summed = lax.psum(partial_value, 'mlp')  43.6 us
  transfers between devices with their start and end apart: 4, of which 4 were waited for; matrix products, arithmetic and copies ran while one was open for 5% of the time, Pallas kernels for 0%

commit v1 on v0

v1 whole, which is shorter than its diff:
```python
import functools

import jax
import jax.numpy as jnp
import numpy as np
from jax import lax
from jax.experimental import pallas as pl
from jax.experimental.pallas import tpu as pltpu
from jax.sharding import PartitionSpec as P

MESH = pl.DeviceIdType.MESH
HD = 128
CONT = 16
NEW = 2
NH = 4
T = CONT * NEW
D = 2048
PREFIX = 4096
TAIL = 64
HW = NH * HD
REQ = 32
MLP = 4
HID = 64
CH = 1024
NCH = PREFIX // CH
NEG = -1e30
SCALE = HD ** -0.5
NT = (((1,), (1,)), ((), ()))
F32 = jnp.float32
BF16 = jnp.bfloat16


def layer_norm(values):
    centre = values - jnp.mean(values, axis=-1, keepdims=True)
    spread = jnp.mean(centre * centre, axis=-1, keepdims=True)
    return centre * lax.rsqrt(spread + 1e-05)


def iota(shape, dim):
    return lax.broadcasted_iota(jnp.int32, shape, dim)


def kernel(
    tok_ref, plen_ref, tlen_ref, tsrc_ref, freq_ref, wscore_ref,
    prefix_hbm, tail_hbm, wqkv_hbm, wout_hbm, wg_hbm, wu_hbm, wd_hbm,
    out_ref, score_ref,
    wqkv, kp, vp, tk, tv, wout, w3, s_buf,
    q_send, q_recv, t_send, t_recv, part, z_send, z_recv,
    g_buf, d_send, d_recv, own_half, r_send, r_recv,
    local_sem, qs, qr, ts, tr, ws, wr, zs, zr, gs, gr, fs, dsem, rs, rr,
):
    r = lax.axis_index("req")
    z = lax.axis_index("mlp")
    core = lax.rem(r, 2)
    chip = r // 2
    up = lax.rem(z + 1, MLP)
    down = lax.rem(z + 3, MLP)

    def local(src, dst, i):
        return pltpu.make_async_copy(src, dst, local_sem.at[i])

    def remote(src, dst, ssem, rsem, req, mlp):
        return pltpu.make_async_remote_copy(
            src_ref=src, dst_ref=dst, send_sem=ssem, recv_sem=rsem,
            device_id=(req, mlp), device_id_type=MESH,
        )

    c_qkv = [local(wqkv_hbm.at[i], wqkv.at[i], i) for i in range(3)]
    c_k = [
        local(prefix_hbm.at[0, 0, pl.ds(c * CH, CH)], kp.at[pl.ds(c * CH, CH)], 3 + c)
        for c in range(NCH)
    ]
    c_v = [
        local(prefix_hbm.at[0, 1, pl.ds(c * CH, CH)], vp.at[pl.ds(c * CH, CH)], 7 + c)
        for c in range(NCH)
    ]
    c_tk = local(tail_hbm.at[:, 0], tk, 11)
    c_tv = local(tail_hbm.at[:, 1], tv, 12)
    c_out = local(wout_hbm, wout, 13)
    hbm3 = (wg_hbm, wu_hbm, wd_hbm)
    c_w = [local(hbm3[m], w3.at[m, z], 14 + m) for m in range(3)]
    for copy in c_qkv + c_k + [c_tk, c_tv] + c_v + [c_out] + c_w:
        copy.start()

    barrier = pltpu.get_barrier_semaphore()

    @pl.loop(1, REQ)
    def _(o):
        pl.semaphore_signal(
            barrier, inc=1, device_id=(lax.rem(r + o, REQ), z), device_id_type=MESH
        )

    for other in (up, down):
        pl.semaphore_signal(barrier, inc=1, device_id=(r, other), device_id_type=MESH)
    pl.semaphore_signal(
        barrier, inc=1, device_id=(r, lax.rem(z + 2, MLP)), device_id_type=MESH
    )
    pl.semaphore_wait(barrier, REQ - 1 + MLP - 1)

    w_sends = []
    for m in range(3):
        a = remote(hbm3[m], w3.at[m, z], ws.at[m, 0], wr.at[m, 0], r, up)
        b = remote(hbm3[m], w3.at[m, z], ws.at[m, 1], wr.at[m, 1], r, down)
        a.start()
        b.start()
        w_sends += [a, b]

    def forward(m):
        lo = remote(w3.at[m, down], w3.at[m, down], ws.at[m, 0], wr.at[m, 0], r, up)
        lo.wait_recv()
        a = remote(
            w3.at[m, down, pl.ds(0, HID // 2)], w3.at[m, down, pl.ds(0, HID // 2)],
            ws.at[m, 2], wr.at[m, 2], r, up,
        )
        a.start()
        hi = remote(w3.at[m, up], w3.at[m, up], ws.at[m, 1], wr.at[m, 1], r, down)
        hi.wait_recv()
        b = remote(
            w3.at[m, up, pl.ds(HID // 2, HID // 2)], w3.at[m, up, pl.ds(HID // 2, HID // 2)],
            ws.at[m, 3], wr.at[m, 3], r, down,
        )
        b.start()
        return [a, b]

    tsrc = tsrc_ref[...]
    tlen = tlen_ref[...]
    held = tsrc == r
    held_col = jnp.sum(held.astype(jnp.int32), axis=1, keepdims=True)
    held_len = jnp.sum(jnp.where(held, tlen, 0), axis=1, keepdims=True)
    held_row = jnp.sum(
        jnp.where(iota((REQ, REQ), 0) == iota((REQ, REQ), 1), held_col, 0), axis=0, keepdims=True
    )
    rank_col = jnp.sum(
        jnp.where(iota((REQ, REQ), 1) < iota((REQ, REQ), 0), held_row, 0), axis=1, keepdims=True
    )
    rank_col = jnp.where(held_col > 0, rank_col, -1)
    rank_l = jnp.sum(
        jnp.where(iota((REQ, 256), 0) == iota((REQ, 256), 1) // 8, rank_col, 0),
        axis=0, keepdims=True,
    )
    len_l = jnp.sum(
        jnp.where(rank_col == iota((REQ, CONT * TAIL), 1) // TAIL, held_len, 0),
        axis=0, keepdims=True,
    )
    src_own = tsrc_ref[pl.ds(r, 1), :]
    src_col = jnp.sum(
        jnp.where(iota((CONT, CONT), 0) == iota((CONT, CONT), 1), src_own, 0),
        axis=1, keepdims=True,
    )
    src_l = jnp.sum(
        jnp.where(iota((CONT, 128), 0) == (iota((CONT, 128), 1) // 2) % CONT, src_col, 0),
        axis=0, keepdims=True,
    )
    src_t = jnp.sum(
        jnp.where((iota((128, CONT), 0) // 2) % CONT == iota((128, CONT), 1), src_own, 0),
        axis=1, keepdims=True,
    )
    rank_t = jnp.sum(
        jnp.where(iota((256, REQ), 0) // 8 == iota((256, REQ), 1),
                  jnp.sum(jnp.where(iota((REQ, REQ), 0) == iota((REQ, REQ), 1), rank_col, 0),
                          axis=0, keepdims=True), 0),
        axis=1, keepdims=True,
    )

    def pair(rows, cols, swapped):
        a, b = (iota((rows, cols), 0), iota((rows, cols), 1))
        if swapped:
            a, b = b, a
        return ((a // NH) % NEW == b % NEW) & (a % NH == b // T), a // 8, (b // 2) % CONT

    own_prefix = plen_ref[r]
    own_tail = tlen_ref[pl.ds(r, 1), :]
    tail_col = jnp.sum(
        jnp.where(iota((T, CONT), 0) // NEW == iota((T, CONT), 1), own_tail, 0),
        axis=1, keepdims=True,
    )
    pos = (own_prefix + tail_col + iota((T, 1), 0) % NEW).astype(F32)
    phase = pos * freq_ref[...]
    cos = jnp.cos(phase)
    sin = jnp.where(iota((T, HD), 1) < HD // 2, -1.0, 1.0) * jnp.sin(phase)

    def rope(v):
        return v * cos + pltpu.roll(v, HD // 2, 1) * sin

    x32 = tok_ref[...].astype(F32)
    normed = layer_norm(x32).astype(BF16)
    c_qkv[0].wait()
    proj = jnp.dot(normed, wqkv[0], preferred_element_type=F32)
    qh = [rope(proj[:, h * HD:(h + 1) * HD]).astype(BF16) for h in range(NH)]

    same, slot, _ = pair(REQ * 8, 128, False)
    sel = jnp.where(same & (src_l == slot), 1.0, 0.0).astype(BF16)
    q_all = jnp.concatenate(qh, axis=0)
    q_send[...] = jnp.dot(sel, q_all, preferred_element_type=F32).reshape(REQ, 8, HD)
    q_recv[r] = q_send[r]

    @pl.loop(1, REQ)
    def _(o):
        peer = lax.rem(r + o, REQ)
        remote(q_send.at[peer], q_recv.at[r], qs.at[peer], qr.at[r], peer, z).start()

    c_qkv[1].wait()
    proj = jnp.dot(normed, wqkv[1], preferred_element_type=F32)
    kh = [rope(proj[:, h * HD:(h + 1) * HD]).astype(BF16) for h in range(NH)]
    c_qkv[2].wait()
    vnew = jnp.dot(normed, wqkv[2], preferred_element_type=F32).astype(BF16)

    row, col = iota((T, T), 0), iota((T, T), 1)
    causal = (row // NEW == col // NEW) & (col <= row)
    s_new, top = [], []
    for h in range(NH):
        s = lax.dot_general(qh[h], kh[h], NT, preferred_element_type=F32) * SCALE
        s = jnp.where(causal, s, NEG)
        s_new.append(s)
        top.append(jnp.max(s, axis=-1, keepdims=True))
    for c in range(NCH):
        c_k[c].wait()
        mask = iota((T, CH), 1) + c * CH < own_prefix
        for h in range(NH):
            s = lax.dot_general(
                qh[h], kp[c * CH:(c + 1) * CH, h * HD:(h + 1) * HD], NT,
                preferred_element_type=F32,
            ) * SCALE
            s = jnp.where(mask, s, NEG)
            s_buf[h, :, c * CH:(c + 1) * CH] = s
            top[h] = jnp.maximum(top[h], jnp.max(s, axis=-1, keepdims=True))

    @pl.loop(1, REQ)
    def _(o):
        peer = lax.rem(r + o, REQ)
        remote(q_send.at[peer], q_recv.at[peer], qs.at[peer], qr.at[peer], peer, z).wait()

    same, slot, kk = pair(128, REQ * 8, True)
    gsel = jnp.where(same & (rank_l == iota((128, 256), 0) // 2 % CONT), 1.0, 0.0).astype(BF16)
    q_t = jnp.dot(
        gsel, q_recv[...].reshape(REQ * 8, HD).astype(BF16), preferred_element_type=F32
    ).astype(BF16)
    c_tk.wait()
    c_tv.wait()
    mine = (iota((T, CONT * TAIL), 0) // NEW == iota((T, CONT * TAIL), 1) // TAIL) & (
        iota((T, CONT * TAIL), 1) % TAIL < len_l
    )
    outs, stats = [], []
    lane = iota((T, HD), 1)
    for h in range(NH):
        keys = tk[:, :, h * HD:(h + 1) * HD].reshape(CONT * TAIL, HD)
        s = lax.dot_general(
            q_t[h * T:(h + 1) * T], keys, NT, preferred_element_type=F32
        ) * SCALE
        s = jnp.where(mine, s, NEG)
        m = jnp.max(s, axis=-1, keepdims=True)
        p = jnp.where(mine, jnp.exp(s - m), 0.0)
        l = jnp.sum(p, axis=-1, keepdims=True)
        values = tv[:, :, h * HD:(h + 1) * HD].reshape(CONT * TAIL, HD)
        outs.append(jnp.dot(p.astype(BF16), values, preferred_element_type=F32))
        stats.append(jnp.where(lane == 0, m, jnp.where(lane == 1, l, 0.0)))
    packed = jnp.concatenate(
        [jnp.concatenate(outs, axis=0), jnp.concatenate(stats, axis=0)], axis=1
    )
    same, slot, kk = pair(REQ * 8, 128, False)
    back = jnp.where(same & (rank_t == kk), 1.0, 0.0)
    t_send[...] = jnp.dot(
        back, packed, preferred_element_type=F32, precision=lax.Precision.HIGHEST
    ).reshape(REQ, 8, 2 * HD)
    t_recv[r] = t_send[r]

    @pl.loop(1, REQ)
    def _(o):
        peer = lax.rem(r + o, REQ)
        remote(t_send.at[peer], t_recv.at[r], ts.at[peer], tr.at[r], peer, z).start()

    w_sends += forward(0)

    acc, total = [], []
    for h in range(NH):
        p = jnp.where(causal, jnp.exp(s_new[h] - top[h]), 0.0)
        total.append(jnp.sum(p, axis=-1, keepdims=True))
        acc.append(
            jnp.dot(p.astype(BF16), vnew[:, h * HD:(h + 1) * HD], preferred_element_type=F32)
        )
    for c in range(NCH):
        c_v[c].wait()
        mask = iota((T, CH), 1) + c * CH < own_prefix
        for h in range(NH):
            p = jnp.where(mask, jnp.exp(s_buf[h, :, c * CH:(c + 1) * CH] - top[h]), 0.0)
            total[h] += jnp.sum(p, axis=-1, keepdims=True)
            acc[h] += jnp.dot(
                p.astype(BF16), vp[c * CH:(c + 1) * CH, h * HD:(h + 1) * HD],
                preferred_element_type=F32,
            )

    w_sends += forward(1)

    @pl.loop(1, REQ)
    def _(o):
        peer = lax.rem(r + o, REQ)
        remote(t_send.at[peer], t_recv.at[peer], ts.at[peer], tr.at[peer], peer, z).wait()

    same, slot, _ = pair(128, REQ * 8, True)
    pick = jnp.where(same & (src_t == slot), 1.0, 0.0)
    got = jnp.dot(
        pick, t_recv[...].reshape(REQ * 8, 2 * HD), preferred_element_type=F32,
        precision=lax.Precision.HIGHEST,
    )
    mix = []
    for h in range(NH):
        part_h = got[h * T:(h + 1) * T]
        m_t, l_t = part_h[:, HD:HD + 1], part_h[:, HD + 1:HD + 2]
        overall = jnp.maximum(top[h], m_t)
        a, b = jnp.exp(top[h] - overall), jnp.exp(m_t - overall)
        mix.append(
            ((a * acc[h] + b * part_h[:, :HD]) / (a * total[h] + b * l_t)).astype(BF16)
        )
    mixed = jnp.concatenate(mix, axis=1)
    c_out.wait()
    part[...] = jnp.dot(mixed, wout[...], preferred_element_type=F32).reshape(MLP, 8, D)
    z_send[...] = part[...].astype(BF16)
    z_copies = []
    for i in range(1, MLP):
        peer = lax.rem(z + i, MLP)
        copy = remote(z_send.at[peer], z_recv.at[i - 1], zs.at[i - 1], zr.at[i - 1], r, peer)
        copy.start()
        z_copies.append(copy)
    w_sends += forward(2)
    summed = part[z]
    for i in range(1, MLP):
        z_copies[i - 1].wait()
        summed += z_recv[i - 1].astype(F32)
    own = tok_ref[pl.ds(pl.multiple_of(z * 8, 8), 8), :].astype(F32)
    residual = (own + summed).astype(BF16).astype(F32)
    normed_mid = layer_norm(residual).astype(BF16)

    me = core * 16 + chip
    g_buf[me] = normed_mid
    sib = r + 1 - 2 * core

    @pl.loop(1, 16)
    def _(o):
        other = lax.rem(chip + o, 16)
        remote(
            g_buf.at[me], g_buf.at[me], gs.at[o], gr.at[me], other * 2 + core, z
        ).start()

    first = remote(g_buf.at[me], g_buf.at[me], fs.at[0], gr.at[me], sib, z)
    first.start()

    @pl.loop(1, 16)
    def _(o):
        theirs = core * 16 + lax.rem(chip + o, 16)
        remote(g_buf.at[theirs], g_buf.at[theirs], gs.at[o], gr.at[theirs], sib, z).wait_recv()
        remote(g_buf.at[theirs], g_buf.at[theirs], fs.at[o], gr.at[theirs], sib, z).start()

    @pl.loop(0, 16)
    def _(o):
        theirs = (1 - core) * 16 + lax.rem(chip + o, 16)
        remote(g_buf.at[theirs], g_buf.at[theirs], fs.at[o], gr.at[theirs], sib, z).wait_recv()

    @pl.loop(0, 16)
    def _(o):
        remote(g_buf.at[me], g_buf.at[me], fs.at[o], gr.at[me], sib, z).wait_send()

    @pl.loop(1, 16)
    def _(o):
        remote(g_buf.at[me], g_buf.at[me], gs.at[o], gr.at[me], sib, z).wait_send()

    opp = lax.rem(z + 2, MLP)
    for m in range(3):
        c_w[m].wait()
        a = w3.at[m, opp, pl.ds(0, HID // 2)]
        b = w3.at[m, opp, pl.ds(HID // 2, HID // 2)]
        remote(a, a, ws.at[m, 2], wr.at[m, 2], r, up).wait_recv()
        remote(b, b, ws.at[m, 3], wr.at[m, 3], r, down).wait_recv()
    for copy in w_sends:
        copy.wait_send()

    def mlp(side):
        rows = g_buf[pl.ds(side * 16, 16)].reshape(128, D)
        wg = w3[0].reshape(MLP * HID, D)
        wu = w3[1].reshape(MLP * HID, D)
        wd = w3[2].reshape(MLP * HID, D)
        gate = lax.dot_general(rows, wg, NT, preferred_element_type=F32)
        upper = lax.dot_general(rows, wu, NT, preferred_element_type=F32)
        hidden = (gate / (1.0 + jnp.exp(-gate)) * upper).astype(BF16)
        return jnp.dot(hidden, wd, preferred_element_type=F32).reshape(16, 8, D)

    d_send[...] = mlp(1 - core).astype(BF16)
    d_copy = remote(d_send, d_recv, dsem.at[0], dsem.at[1], sib, z)
    d_copy.start()
    own_half[...] = mlp(core)
    d_copy.wait()
    own_half[...] += d_recv[...].astype(F32)
    r_send[...] = own_half[...].astype(BF16)

    @pl.loop(1, 16)
    def _(o):
        other = lax.rem(chip + o, 16)
        remote(
            r_send.at[other], r_recv.at[chip], rs.at[o], rr.at[chip], other * 2 + core, z
        ).start()

    r_recv[chip] = jnp.zeros((8, D), BF16)

    @pl.loop(1, 16)
    def _(o):
        other = lax.rem(chip + o, 16)
        remote(
            r_send.at[other], r_recv.at[other], rs.at[o], rr.at[other], other * 2 + core, z
        ).wait()

    layer = residual + own_half[chip]
    for i in range(16):
        layer += r_recv[i].astype(F32)
    out_ref[...] = layer.astype(BF16)
    score_ref[...] = jnp.sum(layer_norm(layer) * wscore_ref[...], axis=-1, keepdims=True)


def on_device(
    tokens, prefix_len, tail_len, tail_src, prefix_kv, tail_kv,
    w_qkv, w_out, w_gate, w_up, w_down, w_score,
):
    exponent = np.arange(HD // 2, dtype=np.float32) * np.float32(2.0 / HD)
    freq = np.power(np.float32(10000.0), -exponent).astype(np.float32)
    freq = jnp.asarray(np.concatenate([freq, freq])[None, :])
    vmem = pl.BlockSpec(memory_space=pltpu.VMEM)
    smem = pl.BlockSpec(memory_space=pltpu.SMEM)
    hbm = pl.BlockSpec(memory_space=pl.ANY)
    dma = pltpu.SemaphoreType.DMA
    out, score = pl.pallas_call(
        kernel,
        out_shape=(
            jax.ShapeDtypeStruct((8, D), BF16),
            jax.ShapeDtypeStruct((8, 1), F32),
        ),
        in_specs=[vmem, smem, vmem, vmem, vmem, vmem] + [hbm] * 7,
        out_specs=(vmem, vmem),
        scratch_shapes=[
            pltpu.VMEM((3, D, HW), BF16),
            pltpu.VMEM((PREFIX, HW), BF16),
            pltpu.VMEM((PREFIX, HW), BF16),
            pltpu.VMEM((CONT, TAIL, HW), BF16),
            pltpu.VMEM((CONT, TAIL, HW), BF16),
            pltpu.VMEM((HW, D), BF16),
            pltpu.VMEM((3, MLP, HID, D), BF16),
            pltpu.VMEM((NH, T, PREFIX), F32),
            pltpu.VMEM((REQ, 8, HD), F32),
            pltpu.VMEM((REQ, 8, HD), F32),
            pltpu.VMEM((REQ, 8, 2 * HD), F32),
            pltpu.VMEM((REQ, 8, 2 * HD), F32),
            pltpu.VMEM((MLP, 8, D), F32),
            pltpu.VMEM((MLP, 8, D), BF16),
            pltpu.VMEM((MLP - 1, 8, D), BF16),
            pltpu.VMEM((REQ, 8, D), BF16),
            pltpu.VMEM((16, 8, D), BF16),
            pltpu.VMEM((16, 8, D), BF16),
            pltpu.VMEM((16, 8, D), F32),
            pltpu.VMEM((16, 8, D), BF16),
            pltpu.VMEM((16, 8, D), BF16),
            dma((17,)),
            dma((REQ,)), dma((REQ,)), dma((REQ,)), dma((REQ,)),
            dma((3, 4)), dma((3, 4)),
            dma((MLP - 1,)), dma((MLP - 1,)),
            dma((16,)), dma((REQ,)), dma((16,)),
            dma((2,)),
            dma((16,)), dma((16,)),
        ],
        compiler_params=pltpu.CompilerParams(
            collective_id=0, has_side_effects=True, vmem_limit_bytes=56 * 1024 * 1024
        ),
        name="layer",
    )(
        tokens, prefix_len, tail_len, tail_src.reshape(REQ, CONT), freq,
        w_score.reshape(1, D),
        prefix_kv, tail_kv, jnp.transpose(w_qkv, (1, 0, 2)), w_out, w_gate, w_up, w_down,
    )
    return out, score.reshape(8)


def solution(mesh):
    in_specs = (
        P("req", None),
        P(),
        P(),
        P(),
        P("req", None, None, "mlp"),
        P("req", None, None, "mlp"),
        P(None, None, "mlp"),
        P("mlp", None),
        P(("req", "mlp"), None),
        P(("req", "mlp"), None),
        P(("req", "mlp"), None),
        P(),
    )
    out_specs = (P(("req", "mlp"), None), P(("req", "mlp")))
    return jax.shard_map(
        on_device, mesh=mesh, in_specs=in_specs, out_specs=out_specs, check_vma=False
    )
```

time: 870 us -> 67.3 us (0.08)
  waiting for transfers between devices: 753 us -> 0 us
  Pallas kernels: 0 us -> 60.9 us
  local copies, waits for them, and re-layouts: 42.8 us -> 4.11 us
  matrix products: 29.6 us -> 0 us
  other arithmetic: 21.2 us -> 1.31 us
  between operations: 14 us -> 0.64 us
    reduce_scatter x1 -> x0, waiting for transfers between devices: 651 us -> none  [on_device(): lax.psum_scatter(swiglu(collected_entries, w_gate, w_up, w_down), ('req',...]
    pallas_call x0 -> x1, Pallas kernels: none -> 60.9 us  [on_device(): pl.pallas_call(kernel, out_shape=(jax.ShapeDtypeStruct((8, D), BF16), jax...]
    all_gather x1 -> x0, waiting for transfers between devices: 46.5 us -> none  [on_device(): collected_entries = lax.all_gather(normed_mid, 'req', axis=0, tiled=True)]
    psum x1 -> x0, waiting for transfers between devices: 43.6 us -> none  [on_device(): summed = lax.psum(partial_value, 'mlp')]
    dot_general x10 -> x0, matrix products: 29.6 us -> none  [the longest x1 7.96 us: swiglu(): return jnp.dot(hidden, down_rows, preferred_element_type=jnp.float32)]
    all_to_all x1 -> x0, waiting for transfers between devices: 12.4 us -> none  [on_device(): lax.all_to_all(outgoing, 'req', split_axis=0, concat_axis=0, tiled=True)]
    reduce_sum x12 -> x0, other arithmetic: 12 us -> none  [the longest x3 3.76 us: attend(): row_sum = jnp.sum(weights, axis=-1)]
    unnamed x22 -> x2, local copies, waits for them, and re-layouts: 12.9 us -> 2.75 us
  transfers between devices with their start and end apart: 4 -> 0, of which waited for: 4 -> 0; matrix products, arithmetic and copies ran while one was open for 5% -> 0% of each run, Pallas kernels for 0% -> 0%
where the time goes in v1:
time: 67.3 us; the launch traced here: 67 us
  Pallas kernels  60.9 us (90%)
  local copies, waits for them, and re-layouts  4.11 us (6%)
  other arithmetic  1.31 us (2%)
    pallas_call x1, Pallas kernels, on_device(): pl.pallas_call(kernel, out_shape=(jax.ShapeDtypeStruct((8, D), BF16), jax...  60.9 us
    unnamed x2, local copies, waits for them, and re-layouts  2.75 us
    reshape x1, local copies, waits for them, and re-layouts, on_device(): tail_src.reshape(REQ, CONT)  1.36 us

profile of v1, /device:TPU:0, one launch (start us, length us, event | category | flops | bytes accessed | tf_op | source)
XLA Modules:
  0.0 67.0 jit_solution(7899312383585347245)
XLA Ops:
  0.6 1.4 %copy.16.tlen_ref = s32[32,16]{1,0:T(8,128)} copy(s32[32,16]{0,1:T(8,128)} %param.15) | data formatting | bytes 4096 | tf_op args[2]
  2.0 1.4 %reshape.13.tsrc_ref = s32[32,16]{1,0:T(8,128)} reshape(s32[512]{0:T(512)} %param.16) | data formatting | bytes 4096 | tf_op jit(solution)/shard_map/reshape | solution.py:471
  3.4 60.9 %layer.1 = (bf16[8,2048]{1,0:T(8,128)(2,1)}, f32[8,1]{1,0:T(8,128)}) custom-call(bf16[32,2048]{1,0:T(8,128)(2,1)} %tok_ref.1, s32[32]{0:T(128)} %plen_ref.1, s32[32,16]{1,0:T(8,128)} %copy.16.tlen_ref, s32[32,16]{1,0:T(8,128)} %reshape.13.tsrc_ref, f32[1,128]{1,0:T(1,128)} %constant.2.clone.freq_ref, f32[1,2048]{1,0:T(1,128)} %bitcast.3, ...), custom_call_target="tpu_custom_call" | custom-call | tf_op jit(solution)/shard_map/layer/pallas_call | solution.py:428
  64.3 1.3 %reduce = f32[8]{0:T(128)} reduce(f32[8,1]{1,0:T(8,128)} %get-tuple-element.5, f32[]{:T(128)} %constant.8), dimensions={1}, to_apply=%get-tuple-element.5.reduce_sub_computation | reduce | bytes 68 | tf_op jit(solution)/shard_map/layer/pallas_call | solution.py:428
  65.6 1.4 %copy.18 = bf16[8,2048]{1,0:T(8,128)(2,1)} copy(bf16[8,2048]{1,0:T(8,128)(2,1)} %get-tuple-element.8) | data formatting | bytes 65536
